TPU v7x, 256 devices: a whole 4x4x8 slice. The times are simulated.
256 devices in a mesh: replica: 8 (over z), tile: 32 (over y, x, core).
Axes of the slice: x: 4, y: 4, z: 8, core: 2. Of those that a mesh axis runs over, the one named last changes fastest.
Arguments:
- fields: bfloat16 [8, 64, 128, 8, 128], P('replica', None, 'tile'), may hold values from -6 to 6
- convolution_weight: bfloat16 [64, 1728], replicated, may hold values from -0.15625 to 0.15625
- convolution_bias: float32 [64], replicated, may hold values from -3 to 3
- query_owner: int32 [8, 4096, 1], P('replica', 'tile'), may hold values from 0 to 31; in each aligned block of 128 rows (0 to 127, 128 to 255, ..., all dimensions but the last counted through in order) at most 8 rows name the same one
- query_cell: int32 [8, 4096], P('replica', 'tile'), may hold values from 0 to 4095
- query_frac: float32 [8, 3, 4096], P('replica', None, 'tile'), may hold values from 0 to 1
- target: float32 [8, 5, 4096], P('replica', None, 'tile'), may hold values from -6 to 6
- w_latent: float32 [64, 512], replicated, may hold values from -3 to 3
- w_pos: float32 [3, 512], replicated, may hold values from -3.5 to 3.5
- bias_one: float32 [512], replicated, may hold values from -2 to 2
- w_mid: float32 [512, 512], replicated, may hold values from -0.5 to 0.5
- bias_two: float32 [512], replicated, may hold values from -2 to 2
- w_out: float32 [5, 512], replicated, may hold values from -0.25 to 0.25
- bias_out: float32 [5], replicated, may hold values from -3 to 3
Outputs:
- prediction: float32 [8, 5, 4096], P('replica', None, 'tile')
- grad_latent: float32 [64, 512], replicated
- grad_pos: float32 [3, 512], replicated
- grad_bias_one: float32 [512], replicated
- grad_mid: float32 [512, 512], replicated
- grad_bias_two: float32 [512], replicated
- grad_out: float32 [5, 512], replicated
- grad_bias_out: float32 [5], replicated
- loss: float32 [], replicated
Inputs may be any that keep to these rules, and one draw needn't show every extreme that they name: `query_owner`: among the query points of one device, no tile is named more than 8 times; in every draw some device names some tile exactly 8 times.
All inputs are finite; a program needn't handle non-finite values.
Results may differ from a plain program's by a relative error of at most 0.0009.
The roundings to bfloat16 on the way count: a program that leaves them out, or rounds other values in their place, can miss the bound.
Values may be sent and summed in bfloat16 or wider, within the bound.
A program may use at most 64 MiB of HBM per device.

v0:
```python
import jax
import jax.numpy as jnp
from jax import lax
from jax.sharding import PartitionSpec as P

DILATION_RATE = 2
VISCOSITY = 0.05
DIFFUSIVITY = 0.05
RESIDUAL_WEIGHT = 0.5


def extended_2(cells, sides, width):
    for axis, dim in sides:
        count = lax.axis_size(axis)
        head = lax.slice_in_dim(cells, 0, width, axis=dim)
        tail = lax.slice_in_dim(cells, cells.shape[dim] - width, cells.shape[dim], axis=dim)
        cells = jnp.concatenate(
            [
                lax.ppermute(tail, axis, [(i, (i + 1) % count) for i in range(count)]),
                cells,
                lax.ppermute(head, axis, [((i + 1) % count, i) for i in range(count)]),
            ],
            axis=dim,
        )
    return cells


def passed_along(value, axis, steps):
    count = lax.axis_size(axis)
    pairs = [(source, (source + steps) % count) for source in range(count)]
    return lax.ppermute(value, axis, pairs)


def corner_index(start_x, start_y, start_z, span_x, span_y, span_z):
    listed = []
    for corner in range(8):
        high_x = corner // 4
        high_y = corner // 2 % 2
        high_z = corner % 2
        listed.append(
            (start_x + high_x) % span_x * (span_y * span_z)
            + (start_y + high_y) % span_y * span_z
            + (start_z + high_z) % span_z
        )
    return jnp.stack(listed, axis=0)


def corner_weight(fraction):
    frac_x, frac_y, frac_z = (fraction[0], fraction[1], fraction[2])
    listed = []
    for corner in range(8):
        part_x = frac_x if corner // 4 == 1 else 1.0 - frac_x
        part_y = frac_y if corner // 2 % 2 == 1 else 1.0 - frac_y
        part_z = frac_z if corner % 2 == 1 else 1.0 - frac_z
        listed.append(part_x * part_y * part_z)
    return jnp.stack(listed, axis=0).astype(jnp.bfloat16)


def tanh_jet(pre_act, tangent, second):
    activation = jnp.tanh(pre_act)
    slope_one = 1.0 - activation * activation
    curvature = -2.0 * activation * slope_one
    return (
        activation,
        slope_one[None] * tangent,
        slope_one[None] * second + curvature[None] * tangent * tangent,
    )


def decode(params, latent_code, position):
    w_latent, w_pos, bias_one, w_mid, bias_two, w_out, bias_out = params
    highest = lax.Precision.HIGHEST
    row_count = latent_code.shape[0]
    hidden_width = w_mid.shape[0]
    first_sum = (
        jnp.dot(latent_code, w_latent, precision=highest)
        + jnp.dot(position, w_pos, precision=highest)
        + bias_one
    )
    tangent = jnp.broadcast_to(w_pos[:, None, :], (3, row_count, hidden_width))
    second = jnp.zeros((3, row_count, hidden_width), jnp.float32)
    activation, tangent, second = tanh_jet(first_sum, tangent, second)
    stacked = jnp.concatenate([activation[None], tangent, second], axis=0).reshape(
        7 * row_count, hidden_width
    )
    mixed_jet = jnp.dot(stacked, w_mid, precision=highest).reshape(7, row_count, hidden_width)
    activation, tangent, second = tanh_jet(mixed_jet[0] + bias_two, mixed_jet[1:4], mixed_jet[4:7])
    stacked = jnp.concatenate([activation[None], tangent, second], axis=0).reshape(
        7 * row_count, hidden_width
    )
    result_jet = jnp.dot(stacked, w_out.T, precision=highest).reshape(7, row_count, 5)
    return (result_jet[0] + bias_out, result_jet[1:4], result_jet[4:7])


def point_loss(params, latent_code, position, target_rows, query_total):
    value, first_jet, second_jet = decode(params, latent_code, position)
    laplace = jnp.sum(second_jet, axis=0)
    velocity = value[:, 2:5]
    advection = jnp.sum(velocity.T[:, :, None] * first_jet, axis=0)
    continuity = first_jet[0][:, 2] + first_jet[1][:, 3] + first_jet[2][:, 4]
    pressure = jnp.stack([first_jet[0][:, 1], first_jet[1][:, 1], first_jet[2][:, 1]], axis=1)
    momentum = advection[:, 2:5] + pressure - VISCOSITY * laplace[:, 2:5]
    momentum = momentum - jnp.concatenate([jnp.zeros_like(value[:, :2]), value[:, 0:1]], axis=1)
    energy = advection[:, 0] - DIFFUSIVITY * laplace[:, 0]
    misfit = jnp.sum((value - target_rows) * (value - target_rows), axis=1)
    physics = continuity * continuity + jnp.sum(momentum * momentum, axis=1) + energy * energy
    return (jnp.sum(misfit + RESIDUAL_WEIGHT * physics) / query_total, value)


def convolved_tile(padded_field, convolution_weight, convolution_bias, border_width, out_planes):
    channels, rows_y, rows_z = (padded_field.shape[0], padded_field.shape[2], padded_field.shape[3])
    summed = jnp.zeros((channels, out_planes * rows_y * rows_z), jnp.float32)
    for spacing_along_y in (-1, 0, 1):
        for spacing_along_z in (-1, 0, 1):
            shifted_field = jnp.roll(
                padded_field, (-spacing_along_y, -spacing_along_z), axis=(2, 3)
            )
            for spacing_along_x in (-1, 0, 1):
                tap_index = (
                    9 * (spacing_along_x + 1) + 3 * (spacing_along_y + 1) + spacing_along_z + 1
                )
                leading_plane = border_width + DILATION_RATE * spacing_along_x
                plane_slab = shifted_field[:, leading_plane : leading_plane + out_planes].reshape(
                    channels, out_planes * rows_y * rows_z
                )
                summed = summed + jnp.dot(
                    convolution_weight[:, tap_index * channels : (tap_index + 1) * channels],
                    plane_slab,
                    preferred_element_type=jnp.float32,
                )
    latent_code = jax.nn.gelu(summed + convolution_bias[:, None]).astype(jnp.bfloat16)
    return latent_code.reshape(channels, out_planes, rows_y, rows_z)


def body(
    fields,
    convolution_weight,
    convolution_bias,
    query_owner,
    query_cell,
    query_frac,
    target,
    w_latent,
    w_pos,
    bias_one,
    w_mid,
    bias_two,
    w_out,
    bias_out,
):
    tile_count = lax.axis_size("tile")
    replica_count = lax.axis_size("replica")
    channels, plane_list, rows_y, rows_z = (
        fields.shape[1],
        fields.shape[2],
        fields.shape[3],
        fields.shape[4],
    )
    local_field = fields[0]
    padded_field = extended_2(local_field, (("tile", 1),), DILATION_RATE)
    latent_code = convolved_tile(
        padded_field, convolution_weight, convolution_bias, DILATION_RATE, plane_list
    )
    upper_plane = passed_along(latent_code[:, :1], "tile", -1)
    extended = jnp.concatenate([latent_code, upper_plane], axis=1)
    plane_span = extended.shape[1]
    flat_latent = extended.reshape(channels, plane_span * rows_y * rows_z)
    owner_tile = query_owner[0, :, 0]
    base_cell = query_cell[0]
    fraction = query_frac[0]
    query_count = owner_tile.shape[0]
    slot_count = 2 * query_count // tile_count
    owner_hits = (owner_tile[:, None] == jnp.arange(tile_count, dtype=jnp.int32)[None, :]).astype(
        jnp.int32
    )
    slot_index = jnp.sum(jnp.cumsum(owner_hits, axis=0) * owner_hits, axis=1) - 1
    base_plane = base_cell // (rows_y * rows_z)
    base_y = base_cell // rows_z % rows_y
    base_z = base_cell % rows_z
    weights = corner_weight(fraction)
    cell_buffer = (
        jnp.zeros((tile_count, 1, slot_count), jnp.int32)
        .at[owner_tile, 0, slot_index]
        .set(base_cell)
    )
    cells_here = lax.all_to_all(cell_buffer, "tile", split_axis=0, concat_axis=0, tiled=True)[:, 0]
    corner_cells = corner_index(
        cells_here // (rows_y * rows_z),
        cells_here // rows_z % rows_y,
        cells_here % rows_z,
        plane_span,
        rows_y,
        rows_z,
    )
    corner_rows = flat_latent[:, corner_cells]
    received = lax.all_to_all(
        jnp.transpose(corner_rows, (2, 0, 1, 3)), "tile", split_axis=0, concat_axis=0, tiled=True
    )
    picked = received[owner_tile, :, :, slot_index]
    interp = jnp.sum(
        picked.astype(jnp.float32) * weights.T.astype(jnp.float32)[:, None, :], axis=2
    ).astype(jnp.bfloat16)
    global_x = owner_tile * plane_list + base_plane
    position = jnp.stack(
        [
            (global_x.astype(jnp.float32) + fraction[0]) / (plane_list * tile_count),
            (base_y.astype(jnp.float32) + fraction[1]) / rows_y,
            (base_z.astype(jnp.float32) + fraction[2]) / rows_z,
        ],
        axis=1,
    )
    target_rows = target[0].T
    query_total = float(query_count * tile_count * replica_count)
    params = (w_latent, w_pos, bias_one, w_mid, bias_two, w_out, bias_out)
    latent_rows = interp.astype(jnp.float32)

    def local_loss(weights_all):
        return point_loss(weights_all, latent_rows, position, target_rows, query_total)

    loss_value, pullback, value = jax.vjp(local_loss, params, has_aux=True)
    gradients = pullback(jnp.ones((), jnp.float32))[0]
    summed = lax.psum(
        (
            gradients[0],
            gradients[1],
            gradients[2],
            gradients[3],
            gradients[4],
            gradients[5],
            gradients[6],
            loss_value,
        ),
        ("replica", "tile"),
    )
    return (
        value.T[None],
        summed[0],
        summed[1],
        summed[2],
        summed[3],
        summed[4],
        summed[5],
        summed[6],
        summed[7],
    )


def solution(mesh):
    return jax.shard_map(
        body,
        mesh=mesh,
        in_specs=(
            P("replica", None, "tile", None, None),
            P(),
            P(),
            P("replica", "tile", None),
            P("replica", "tile"),
            P("replica", None, "tile"),
            P("replica", None, "tile"),
            P(),
            P(),
            P(),
            P(),
            P(),
            P(),
            P(),
        ),
        out_specs=(P("replica", None, "tile"), P(), P(), P(), P(), P(), P(), P(), P()),
        check_vma=False,
    )
```

profile of v0, /device:TPU:8, one launch (start us, length us, event | category | flops | bytes accessed | tf_op | source)
XLA Modules:
  0.0 412.3 jit_solution(445695020267430060)
XLA Ops:
  8.5 3.8 collective-permute-start.1
  14.8 10.9 %scatter_fusion = s32[32,8]{0,1:T(8,128)S(1)} fusion(s32[32,8]{0,1:T(8,128)S(1)} %broadcast.5262, s32[128]{0:T(128)S(1)} %get-tuple-element.71, s32[128]{0:T(128)} %bitcast.586), kind=kCustom, calls=%fused_computation.2 | custom fusion | bytes 2560 | tf_op jit(solution)/shard_map/scatter | solution.py:184
  26.4 6.9 %all-to-all-start = ((s32[32,1,8]{2,1,0:T(1,128)}), s32[32,1,8]{2,1,0:T(1,128)S(1)}, u32[]{:S(2)}, u32[]{:S(2)}) async-start(s32[32,1,8]{2,1,0:T(1,128)} %copy.65), calls=%async_computation | async-start | bytes 32768 | tf_op jit(solution)/shard_map/all_to_all | solution.py:186
  33.6 5.8 %all-to-all-done = s32[32,1,8]{2,1,0:T(1,128)S(1)} async-done(((s32[32,1,8]{2,1,0:T(1,128)}), s32[32,1,8]{2,1,0:T(1,128)S(1)}, u32[]{:S(2)}, u32[]{:S(2)}) %all-to-all-start) | async-done | bytes 1056 | tf_op jit(solution)/shard_map/all_to_all | solution.py:186
  41.4 2.9 fusion.26
  44.3 1.8 fusion.27
  46.1 1.9 fusion.49
  54.5 1.7 fusion.44
  65.9 1.6 collective-permute-start.2
  67.4 2.5 collective-permute-done.2
  71.1 6.2 %gather_fusion = bf16[2048,64]{1,0:T(8,128)(2,1)S(1)} fusion(bf16[64,5120]{0,1:T(8,128)(2,1)S(1)} %bitcast.530, s32[2048]{0:T(1024)S(1)} %broadcast_clamp_fusion), kind=kCustom, calls=%fused_computation | custom fusion | bytes 532480 | tf_op jit(solution)/shard_map/gather | solution.py:195
  79.1 7.7 %all-to-all-start.1 = ((bf16[32,2,2048]{2,1,0:T(2,128)(2,1)}), bf16[32,2,2048]{2,1,0:T(2,128)(2,1)S(1)}, u32[]{:S(2)}, u32[]{:S(2)}) async-start(bf16[32,2,2048]{2,1,0:T(2,128)(2,1)} %reshape.1907), calls=%async_computation.1 | async-start | bytes 524288 | tf_op jit(solution)/shard_map/all_to_all | solution.py:196
  87.5 6.8 %all-to-all-done.1 = bf16[32,2,2048]{2,1,0:T(2,128)(2,1)S(1)} async-done(((bf16[32,2,2048]{2,1,0:T(2,128)(2,1)}), bf16[32,2,2048]{2,1,0:T(2,128)(2,1)S(1)}, u32[]{:S(2)}, u32[]{:S(2)}) %all-to-all-start.1) | async-done | bytes 262176 | tf_op jit(solution)/shard_map/all_to_all | solution.py:196
  98.3 2.2 copy.81
  100.5 4.5 %fusion.213 = f32[896,512]{1,0:T(8,128)S(1)} fusion(f32[896,512]{1,0:T(8,128)} %bitcast.538, f32[512,512]{1,0:T(8,128)S(1)} %copy-done), kind=kOutput, calls=%fused_computation.422 | convolution fusion | flops 2818572288 | bytes 4718592 | tf_op jit(solution)/shard_map/jvp()/dot_general | solution.py:86
  108.0 1.6 fusion.214
  112.5 1.6 fusion.113
  117.5 3.1 fusion.215
  120.5 1.3 fusion.200
  121.8 2.3 copy.82
  124.1 1.9 multiply_reduce_fusion.1
  126.0 6.4 %convolution_bitcast_fusion.13 = f32[512,512]{1,0:T(8,128)} fusion(f32[1,128,512]{2,1,0:T(8,128)} %bitcast.580, f32[3,128,512]{2,1,0:T(8,128)} %copy-done.10, f32[3,128,512]{2,1,0:T(8,128)} %copy-done.11, f32[3,128,512]{1,2,0:T(8,128)} %copy-done.9, f32[3,128,512]{1,2,0:T(8,128)} %copy-done.8, f32[1,128,512]{1,2,0:T(8,128)} %copy-done.17), kind=kOutput, calls=%fused_computation.60 | convolution fusion | flops 2820407296 | bytes 4718592 | tf_op jit(solution)/shard_map/transpose(jvp())/dot_general | solution.py:86
  132.4 2.3 copy.84
  134.7 2.8 fusion.37
  137.5 1.8 copy.83
  139.2 1.8 copy.85
  141.1 1.4 fusion.197
  144.7 2.3 convolution_bitcast_fusion.14
  147.3 77.7 %all-reduce.25 = (f32[3,512]{1,0:T(4,128)}, f32[512]{0:T(512)}, f32[512]{0:T(512)}, f32[5,512]{1,0:T(8,128)}, f32[5]{0:T(128)}, /*index=5*/f32[]{:T(128)}) all-reduce(f32[3,512]{1,0:T(4,128)S(1)} %convolution_add_fusion.14, f32[512]{0:T(512)S(1)} %get-tuple-element.67, ...), channel_id=1, replica_groups=mesh['replica'=8,'tile'=32] {'replica','tile'}, use_global_device_ids=true, to_apply=%region_15.16 | all-reduce | flops 5126 | bytes 41008 | tf_op jit(solution)/shard_map/psum | solution.py:222
  225.0 176.5 %all-reduce.29.cloned.1.call-done = (f32[64,512]{1,0:T(8,128)}, f32[512,512]{1,0:T(8,128)}) async-done(((f32[64,512]{1,0:T(8,128)}, f32[512,512]{1,0:T(8,128)}), (f32[64,512]{1,0:T(8,128)}, f32[512,512]{1,0:T(8,128)})) %all-reduce.29.cloned.1.call-update) | async-done | bytes 1179664 | tf_op jit(solution)/shard_map/psum | solution.py:222
  401.4 1.6 copy.245
  403.0 2.3 copy.246
  (200 shorter events, 40.5 us)
Async XLA Ops:
  7.2 93.3 %copy-start = (f32[512,512]{1,0:T(8,128)S(1)}, f32[512,512]{1,0:T(8,128)}, u32[]{:S(2)}) copy-start(f32[512,512]{1,0:T(8,128)} %param.24) | copy-start | bytes 3145732
  7.2 26.2 %copy-start.1 = (bf16[1,64,4,8,128]{4,3,2,1,0:T(8,128)(2,1)S(1)}, bf16[1,64,4,8,128]{4,3,2,1,0:T(8,128)(2,1)}, u32[]{:S(2)}) copy-start(bf16[1,64,4,8,128]{4,3,2,1,0:T(8,128)(2,1)} %param.14) | copy-start | bytes 1572868
  7.2 26.1 %copy-start.25 = (f32[1,3,128]{2,0,1:T(1,128)S(1)}, f32[1,3,128]{2,0,1:T(1,128)}, u32[]{:S(2)}) copy-start(f32[1,3,128]{2,0,1:T(1,128)} %param.19) | copy-start | bytes 4612
  8.4 32.0 %collective-permute-start = (bf16[64,2,8,128]{3,2,1,0:T(8,128)(2,1)S(1)}, bf16[64,2,8,128]{3,2,1,0:T(8,128)(2,1)S(1)}, u32[]{:S(2)}, u32[]{:S(2)}) collective-permute-start(bf16[64,2,8,128]{3,2,1,0:T(8,128)(2,1)S(1)} %get-tuple-element.124), channel_id=1, source_target_pairs={{0,1},{1,2},{2,3},{3,4},{4,5},{5,6},{6,7},{7,8},{8,9},{9,10},{10,1... | collective-permute-start | bytes 786440 | tf_op jit(solution)/shard_map/ppermute | solution.py:19
  8.5 31.9 %collective-permute-start.1 = (bf16[64,2,8,128]{3,2,1,0:T(8,128)(2,1)S(1)}, bf16[64,2,8,128]{3,2,1,0:T(8,128)(2,1)S(1)}, u32[]{:S(2)}, u32[]{:S(2)}) collective-permute-start(bf16[64,2,8,128]{3,2,1,0:T(8,128)(2,1)S(1)} %get-tuple-element.125), channel_id=1, source_target_pairs={{1,0},{2,1},{3,2},{4,3},{5,4},{6,5},{7,6},{8,7},{9,8},{10,9},{11,1... | collective-permute-start | bytes 786440 | tf_op jit(solution)/shard_map/ppermute | solution.py:21
  26.4 13.1 %all-to-all-start = ((s32[32,1,8]{2,1,0:T(1,128)}), s32[32,1,8]{2,1,0:T(1,128)S(1)}, u32[]{:S(2)}, u32[]{:S(2)}) async-start(s32[32,1,8]{2,1,0:T(1,128)} %copy.65), calls=%async_computation | async-start | bytes 32768 | tf_op jit(solution)/shard_map/all_to_all | solution.py:186
  50.3 0.9 copy-start.21
  65.9 4.1 collective-permute-start.2
  77.3 9.6 %copy-start.27 = (s32[1,128,1]{1,2,0:T(1,128)S(1)}, s32[1,128,1]{1,2,0:T(1,128)}, u32[]{:S(2)}) copy-start(s32[1,128,1]{1,2,0:T(1,128)} %param.17) | copy-start | bytes 1540
  77.3 9.5 %copy-start.31 = (s32[1,128]{1,0:T(1,128)S(1)}, s32[1,128]{1,0:T(1,128)}, u32[]{:S(2)}) copy-start(s32[1,128]{1,0:T(1,128)} %param.18) | copy-start | bytes 1540
  77.4 9.7 %copy-start.23 = (f32[3,512]{1,0:T(4,128)S(1)}, f32[3,512]{1,0:T(4,128)}, u32[]{:S(2)}) copy-start(f32[3,512]{1,0:T(4,128)} %param.22) | copy-start | bytes 18436
  79.1 15.2 %all-to-all-start.1 = ((bf16[32,2,2048]{2,1,0:T(2,128)(2,1)}), bf16[32,2,2048]{2,1,0:T(2,128)(2,1)S(1)}, u32[]{:S(2)}, u32[]{:S(2)}) async-start(bf16[32,2,2048]{2,1,0:T(2,128)(2,1)} %reshape.1907), calls=%async_computation.1 | async-start | bytes 524288 | tf_op jit(solution)/shard_map/all_to_all | solution.py:196
  86.8 314.6 %all-reduce.29.cloned.1.call-start = ((), (), s32[]{:S(2)}) async-start(), calls=%async_computation.2 | async-start | bytes 2359296 | tf_op jit(solution)/shard_map/psum | solution.py:222
  94.7 1.2 copy-start.22
  94.7 1.2 copy-start.30
  96.7 1.6 copy-start.17
  97.0 1.1 copy-start.9
  105.7 1.1 copy-start.4
  105.8 1.1 copy-start.18
  106.8 0.9 copy-start.6
  106.8 1.2 copy-start.7
  106.9 1.1 copy-start.24
  108.0 1.6 copy-start.28
  108.0 3.6 copy-start.29
  114.2 1.1 copy-start.3
  114.2 1.4 copy-start.5
  116.1 0.9 copy-start.10
  116.1 1.2 copy-start.11
  116.3 1.1 copy-start.20
  126.0 8.7 %copy-start.13 = (f32[128,512]{0,1:T(8,128)S(1)}, f32[128,512]{0,1:T(8,128)}, u32[]{:S(2)}) copy-start(f32[128,512]{0,1:T(8,128)} %copy-done.12) | copy-start | bytes 786436
  126.0 8.7 %copy-start.15 = (f32[128,512]{0,1:T(8,128)S(1)}, f32[128,512]{0,1:T(8,128)}, u32[]{:S(2)}) copy-start(f32[128,512]{0,1:T(8,128)} %copy-done.14) | copy-start | bytes 786436
  139.2 5.4 %copy-start.19 = (f32[1,128,512]{2,1,0:T(8,128)S(1)}, f32[1,128,512]{2,1,0:T(8,128)}, u32[]{:S(2)}) copy-start(f32[1,128,512]{2,1,0:T(8,128)} %copy-done.18) | copy-start | bytes 786436
  (7 other events, 5.4 us)
Sparse Core Ops, SparseCore 0:
  143.5 257.9 all-reduce.28
where the time goes:
time: 420 us; the launch traced here: 412 us
  waiting for transfers between devices  192 us (46%)
  blocking collectives  77.7 us (18%)
  local copies, waits for them, and re-layouts  50.4 us (12%)
  matrix products  31.4 us (7%)
  other arithmetic  25 us (6%)
  starting transfers between devices  20.2 us (5%)
  between operations  15.9 us (4%)
    psum x1, waiting for transfers between devices, body(): lax.psum((gradients[0], gradients[1], gradients[2], gradients[3], gradien...  176 us
    psum x1, blocking collectives, body(): lax.psum((gradients[0], gradients[1], gradients[2], gradients[3], gradien...  77.7 us
    dot_general x3, matrix products, decode(): jnp.dot(stacked, w_mid, precision=highest)  14 us
    concatenate x8, other arithmetic, convolved_tile(): jnp.roll(padded_field, (-spacing_along_y, -spacing_along_z), axis=(2, 3))  12.2 us
    unnamed x79, local copies, waits for them, and re-layouts  12 us
    scatter x2, local copies, waits for them, and re-layouts, body(): cell_buffer = jnp.zeros((tile_count, 1, slot_count), jnp.int32).at[owner_...  11.6 us
    dot_general x27, matrix products, convolved_tile(): jnp.dot(convolution_weight[:, tap_index * channels:(tap_index + 1) * chan...  9.92 us
  transfers between devices with their start and end apart: 6, of which 4 were waited for; matrix products, arithmetic and copies ran while one was open for 5% of the time, Pallas kernels for 0%

commit v1 on v0

--- a/solution.py
+++ b/solution.py
@@ -220,17 +220,20 @@
     loss_value, pullback, value = jax.vjp(local_loss, params, has_aux=True)
     gradients = pullback(jnp.ones((), jnp.float32))[0]
     summed = lax.psum(
-        (
-            gradients[0],
-            gradients[1],
-            gradients[2],
-            gradients[3],
-            gradients[4],
-            gradients[5],
-            gradients[6],
-            loss_value,
+        lax.psum(
+            (
+                gradients[0],
+                gradients[1],
+                gradients[2],
+                gradients[3],
+                gradients[4],
+                gradients[5],
+                gradients[6],
+                loss_value,
+            ),
+            "replica",
         ),
-        ("replica", "tile"),
+        "tile",
     )
     return (
         value.T[None],

time: 420 us -> 391 us (0.931)
  the two profiles are of different devices: /device:TPU:8 before, /device:TPU:0 now
where the time goes in v1:
time: 391 us; the launch traced here: 384 us
  blocking collectives  153 us (39%)
  waiting for transfers between devices  92.2 us (24%)
  local copies, waits for them, and re-layouts  50.4 us (13%)
  matrix products  30.1 us (8%)
  other arithmetic  25 us (6%)
  starting transfers between devices  17.2 us (4%)
  between operations  15.9 us (4%)
    psum x1, blocking collectives, body(): lax.psum(lax.psum((gradients[0], gradients[1], gradients[2], gradients[3]...  124 us
    psum x1, waiting for transfers between devices, body(): lax.psum((gradients[0], gradients[1], gradients[2], gradients[3], gradien...  74.5 us
    psum x1, blocking collectives, body(): lax.psum((gradients[0], gradients[1], gradients[2], gradients[3], gradien...  29.2 us
    dot_general x3, matrix products, decode(): jnp.dot(stacked, w_mid, precision=highest)  14 us
    concatenate x8, other arithmetic, convolved_tile(): jnp.roll(padded_field, (-spacing_along_y, -spacing_along_z), axis=(2, 3))  12.2 us
    unnamed x83, local copies, waits for them, and re-layouts  12 us
    scatter x2, local copies, waits for them, and re-layouts, body(): cell_buffer = jnp.zeros((tile_count, 1, slot_count), jnp.int32).at[owner_...  11.6 us
    dot_general x27, matrix products, convolved_tile(): jnp.dot(convolution_weight[:, tap_index * channels:(tap_index + 1) * chan...  9.93 us
  transfers between devices with their start and end apart: 7, of which 4 were waited for; matrix products, arithmetic and copies ran while one was open for 5% of the time, Pallas kernels for 0%

profile of v1, /device:TPU:0, one launch (start us, length us, event | category | flops | bytes accessed | tf_op | source)
XLA Modules:
  0.0 383.9 jit_solution(4062163821619677312)
XLA Ops:
  8.5 5.1 %collective-permute-start.1 = (bf16[64,2,8,128]{3,2,1,0:T(8,128)(2,1)S(1)}, bf16[64,2,8,128]{3,2,1,0:T(8,128)(2,1)S(1)}, u32[]{:S(2)}, u32[]{:S(2)}) collective-permute-start(bf16[64,2,8,128]{3,2,1,0:T(8,128)(2,1)S(1)} %get-tuple-element.133), channel_id=1, source_target_pairs={{1,0},{2,1},{3,2},{4,3},{5,4},{6,5},{7,6},{8,7},{9,8},{10,9},{11,1... | collective-permute-start | bytes 786440 | tf_op jit(solution)/shard_map/ppermute | solution.py:21
  16.0 10.9 %scatter_fusion = s32[32,8]{0,1:T(8,128)S(1)} fusion(s32[32,8]{0,1:T(8,128)S(1)} %broadcast.5262, s32[128]{0:T(128)S(1)} %get-tuple-element.79, s32[128]{0:T(128)} %bitcast.586), kind=kCustom, calls=%fused_computation.2 | custom fusion | bytes 2560 | tf_op jit(solution)/shard_map/scatter | solution.py:184
  27.6 3.8 all-to-all-start
  31.8 7.0 %all-to-all-done = s32[32,1,8]{2,1,0:T(1,128)S(1)} async-done(((s32[32,1,8]{2,1,0:T(1,128)}), s32[32,1,8]{2,1,0:T(1,128)S(1)}, u32[]{:S(2)}, u32[]{:S(2)}) %all-to-all-start) | async-done | bytes 1056 | tf_op jit(solution)/shard_map/all_to_all | solution.py:186
  40.6 2.9 fusion.26
  43.5 1.8 fusion.27
  45.3 1.9 fusion.49
  53.7 1.7 fusion.44
  65.1 1.3 collective-permute-start.2
  66.4 2.5 collective-permute-done.2
  70.1 6.2 %gather_fusion = bf16[2048,64]{1,0:T(8,128)(2,1)S(1)} fusion(bf16[64,5120]{0,1:T(8,128)(2,1)S(1)} %bitcast.530, s32[2048]{0:T(1024)S(1)} %broadcast_clamp_fusion), kind=kCustom, calls=%fused_computation | custom fusion | bytes 532480 | tf_op jit(solution)/shard_map/gather | solution.py:195
  78.0 6.8 %all-to-all-start.1 = ((bf16[32,2,2048]{2,1,0:T(2,128)(2,1)}), bf16[32,2,2048]{2,1,0:T(2,128)(2,1)S(1)}, u32[]{:S(2)}, u32[]{:S(2)}) async-start(bf16[32,2,2048]{2,1,0:T(2,128)(2,1)} %reshape.1907), calls=%async_computation.1 | async-start | bytes 524288 | tf_op jit(solution)/shard_map/all_to_all | solution.py:196
  85.5 8.3 %all-to-all-done.1 = bf16[32,2,2048]{2,1,0:T(2,128)(2,1)S(1)} async-done(((bf16[32,2,2048]{2,1,0:T(2,128)(2,1)}), bf16[32,2,2048]{2,1,0:T(2,128)(2,1)S(1)}, u32[]{:S(2)}, u32[]{:S(2)}) %all-to-all-start.1) | async-done | bytes 262176 | tf_op jit(solution)/shard_map/all_to_all | solution.py:196
  97.8 2.2 copy.81
  100.0 4.5 %fusion.213 = f32[896,512]{1,0:T(8,128)S(1)} fusion(f32[896,512]{1,0:T(8,128)} %bitcast.538, f32[512,512]{1,0:T(8,128)S(1)} %copy-done), kind=kOutput, calls=%fused_computation.422 | convolution fusion | flops 2818572288 | bytes 4718592 | tf_op jit(solution)/shard_map/jvp()/dot_general | solution.py:86
  107.5 1.6 fusion.214
  112.0 1.6 fusion.113
  116.9 3.1 fusion.215
  120.0 1.3 fusion.200
  121.2 2.3 copy.82
  123.5 1.9 multiply_reduce_fusion.1
  125.4 6.4 %convolution_bitcast_fusion.13 = f32[512,512]{1,0:T(8,128)} fusion(f32[1,128,512]{2,1,0:T(8,128)} %bitcast.580, f32[3,128,512]{2,1,0:T(8,128)} %copy-done.12, f32[3,128,512]{2,1,0:T(8,128)} %copy-done.13, f32[3,128,512]{1,2,0:T(8,128)} %copy-done.11, f32[3,128,512]{1,2,0:T(8,128)} %copy-done.10, f32[1,128,512]{1,2,0:T(8,128)} %copy-done.19), kind=kOutput, calls=%fused_computation.60 | convolution fusion | flops 2820407296 | bytes 4718592 | tf_op jit(solution)/shard_map/transpose(jvp())/dot_general | solution.py:86
  131.8 2.3 copy.84
  134.1 2.8 fusion.37
  136.9 1.8 copy.83
  138.7 1.8 copy.85
  140.5 1.4 fusion.197
  142.9 74.5 %all-reduce.34.cloned.1.call-done = (f32[64,512]{1,0:T(8,128)}, f32[512,512]{1,0:T(8,128)}) async-done(((f32[64,512]{1,0:T(8,128)}, f32[512,512]{1,0:T(8,128)}), (f32[64,512]{1,0:T(8,128)}, f32[512,512]{1,0:T(8,128)})) %all-reduce.34.cloned.1.call-update) | async-done | bytes 1179664 | tf_op jit(solution)/shard_map/psum | solution.py:223
  219.9 29.2 %all-reduce.27 = (f32[3,512]{1,0:T(4,128)S(1)}, f32[512]{0:T(512)S(1)}, f32[512]{0:T(512)S(1)}, f32[5,512]{1,0:T(8,128)S(1)}, f32[5]{0:T(128)S(1)}, /*index=5*/f32[]{:T(128)}) all-reduce(f32[3,512]{1,0:T(4,128)S(1)} %convolution_add_fusion.14, f32[512]{0:T(512)S(1)} %get-tuple-element.75, ...), channel_id=1, replica_groups=mesh['replica'=8,'tile'=32] {'replica'}, use_global_device_ids=true, to_apply=%region_16.17 | all-reduce | flops 5126 | bytes 41008 | tf_op jit(solution)/shard_map/psum | solution.py:223
  249.1 123.9 %all-reduce.25 = (f32[3,512]{1,0:T(4,128)}, f32[512]{0:T(512)}, f32[512]{0:T(512)}, f32[5,512]{1,0:T(8,128)}, f32[5]{0:T(128)}, /*index=5*/f32[]{:T(128)}) all-reduce(f32[3,512]{1,0:T(4,128)S(1)} %get-tuple-element.61, f32[512]{0:T(512)S(1)} %get-tuple-element.62, ...), channel_id=1, replica_groups=mesh['replica'=8,'tile'=32] {'tile'}, use_global_device_ids=true, to_apply=%region_17.18 | all-reduce | flops 5126 | bytes 41008 | tf_op jit(solution)/shard_map/psum | solution.py:222
  373.0 1.6 copy.247
  374.6 2.3 copy.248
  (208 shorter events, 41.5 us)
Async XLA Ops:
  7.2 92.8 %copy-start = (f32[512,512]{1,0:T(8,128)S(1)}, f32[512,512]{1,0:T(8,128)}, u32[]{:S(2)}) copy-start(f32[512,512]{1,0:T(8,128)} %param.24) | copy-start | bytes 3145732
  7.2 24.3 %copy-start.1 = (bf16[1,64,4,8,128]{4,3,2,1,0:T(8,128)(2,1)S(1)}, bf16[1,64,4,8,128]{4,3,2,1,0:T(8,128)(2,1)}, u32[]{:S(2)}) copy-start(bf16[1,64,4,8,128]{4,3,2,1,0:T(8,128)(2,1)} %param.14) | copy-start | bytes 1572868
  7.2 24.2 %copy-start.27 = (f32[1,3,128]{2,0,1:T(1,128)S(1)}, f32[1,3,128]{2,0,1:T(1,128)}, u32[]{:S(2)}) copy-start(f32[1,3,128]{2,0,1:T(1,128)} %param.19) | copy-start | bytes 4612
  8.4 31.2 %collective-permute-start = (bf16[64,2,8,128]{3,2,1,0:T(8,128)(2,1)S(1)}, bf16[64,2,8,128]{3,2,1,0:T(8,128)(2,1)S(1)}, u32[]{:S(2)}, u32[]{:S(2)}) collective-permute-start(bf16[64,2,8,128]{3,2,1,0:T(8,128)(2,1)S(1)} %get-tuple-element.132), channel_id=1, source_target_pairs={{0,1},{1,2},{2,3},{3,4},{4,5},{5,6},{6,7},{7,8},{8,9},{9,10},{10,1... | collective-permute-start | bytes 786440 | tf_op jit(solution)/shard_map/ppermute | solution.py:19
  8.5 31.1 %collective-permute-start.1 = (bf16[64,2,8,128]{3,2,1,0:T(8,128)(2,1)S(1)}, bf16[64,2,8,128]{3,2,1,0:T(8,128)(2,1)S(1)}, u32[]{:S(2)}, u32[]{:S(2)}) collective-permute-start(bf16[64,2,8,128]{3,2,1,0:T(8,128)(2,1)S(1)} %get-tuple-element.133), channel_id=1, source_target_pairs={{1,0},{2,1},{3,2},{4,3},{5,4},{6,5},{7,6},{8,7},{9,8},{10,9},{11,1... | collective-permute-start | bytes 786440 | tf_op jit(solution)/shard_map/ppermute | solution.py:21
  27.6 11.1 %all-to-all-start = ((s32[32,1,8]{2,1,0:T(1,128)}), s32[32,1,8]{2,1,0:T(1,128)S(1)}, u32[]{:S(2)}, u32[]{:S(2)}) async-start(s32[32,1,8]{2,1,0:T(1,128)} %copy.65), calls=%async_computation | async-start | bytes 32768 | tf_op jit(solution)/shard_map/all_to_all | solution.py:186
  65.1 3.8 collective-permute-start.2
  76.3 8.7 %copy-start.29 = (s32[1,128,1]{1,2,0:T(1,128)S(1)}, s32[1,128,1]{1,2,0:T(1,128)}, u32[]{:S(2)}) copy-start(s32[1,128,1]{1,2,0:T(1,128)} %param.17) | copy-start | bytes 1540
  76.3 8.7 %copy-start.33 = (s32[1,128]{1,0:T(1,128)S(1)}, s32[1,128]{1,0:T(1,128)}, u32[]{:S(2)}) copy-start(s32[1,128]{1,0:T(1,128)} %param.18) | copy-start | bytes 1540
  76.3 8.8 %copy-start.25 = (f32[3,512]{1,0:T(4,128)S(1)}, f32[3,512]{1,0:T(4,128)}, u32[]{:S(2)}) copy-start(f32[3,512]{1,0:T(4,128)} %param.22) | copy-start | bytes 18436
  78.0 15.8 %all-to-all-start.1 = ((bf16[32,2,2048]{2,1,0:T(2,128)(2,1)}), bf16[32,2,2048]{2,1,0:T(2,128)(2,1)S(1)}, u32[]{:S(2)}, u32[]{:S(2)}) async-start(bf16[32,2,2048]{2,1,0:T(2,128)(2,1)} %reshape.1907), calls=%async_computation.1 | async-start | bytes 524288 | tf_op jit(solution)/shard_map/all_to_all | solution.py:196
  84.9 132.5 %all-reduce.34.cloned.1.call-start = ((), (), s32[]{:S(2)}) async-start(), calls=%async_computation.3 | async-start | bytes 2359296 | tf_op jit(solution)/shard_map/psum | solution.py:223
  94.1 1.2 copy-start.24
  94.1 1.2 copy-start.32
  96.2 1.6 copy-start.19
  96.5 1.2 copy-start.11
  105.2 1.1 copy-start.4
  105.3 1.1 copy-start.20
  106.4 1.1 copy-start.8
  106.4 1.1 copy-start.26
  107.5 1.6 copy-start.30
  107.5 3.6 copy-start.31
  113.7 1.1 copy-start.3
  113.7 1.4 copy-start.5
  115.6 1.1 copy-start.13
  115.8 1.1 copy-start.22
  125.4 8.7 %copy-start.15 = (f32[128,512]{0,1:T(8,128)S(1)}, f32[128,512]{0,1:T(8,128)}, u32[]{:S(2)}) copy-start(f32[128,512]{0,1:T(8,128)} %copy-done.14) | copy-start | bytes 786436
  125.4 8.7 %copy-start.17 = (f32[128,512]{0,1:T(8,128)S(1)}, f32[128,512]{0,1:T(8,128)}, u32[]{:S(2)}) copy-start(f32[128,512]{0,1:T(8,128)} %copy-done.16) | copy-start | bytes 786436
  140.5 78.2 %copy-start.21 = (f32[1,128,512]{2,1,0:T(8,128)S(1)}, f32[1,128,512]{2,1,0:T(8,128)}, u32[]{:S(2)}) copy-start(f32[1,128,512]{2,1,0:T(8,128)} %copy-done.20) | copy-start | bytes 786436
  141.9 76.8 %copy-start.7 = (f32[3,128,512]{2,1,0:T(8,128)S(1)}, f32[3,128,512]{2,1,0:T(8,128)}, u32[]{:S(2)}) copy-start(f32[3,128,512]{2,1,0:T(8,128)} %copy-done.6) | copy-start | bytes 2359300
  141.9 76.8 %copy-start.9 = (f32[3,128,512]{2,1,0:T(8,128)S(1)}, f32[3,128,512]{2,1,0:T(8,128)}, u32[]{:S(2)}) copy-start(f32[3,128,512]{2,1,0:T(8,128)} %copy-done.8) | copy-start | bytes 2359300
  142.8 230.2 %all-reduce.32.cloned.1.call-start = ((), (), s32[]{:S(2)}) async-start(), calls=%async_computation.2 | async-start | bytes 2359296 | tf_op jit(solution)/shard_map/psum | solution.py:222
  (10 other events, 8.1 us)
Sparse Core Ops, SparseCore 0:
  143.0 74.3 all-reduce.33
  220.7 113.7 all-reduce.31
